TPU v7x, 32 devices: a whole 2x2x4 slice. The times are simulated.
32 devices in a mesh: chan: 4 (over x, core), pix: 8 (over z, y).
Axes of the slice: x: 2, y: 2, z: 4, core: 2. Of those that a mesh axis runs over, the one named last changes fastest.
Arguments:
- sky_map: bfloat16 [1024, 256, 1024], P('chan', 'pix'), may hold values from -6 to 6
- owner: int32 [256], P('pix'), may hold values from -1 to 3, as said below
- stamp_block: int32 [8, 4, 8, 2], P('pix', 'chan'), may hold values from -1 to 5, as said below
- chan_start: int32 [8, 4, 8, 2], P('pix', 'chan'), may hold values from 0 to 896
- overdensity: float32 [8, 4, 8, 2], replicated, may hold values from 0.2 to 3
- delay_gain: float32 [1024], replicated, may hold values from 0.1 to 1
Outputs:
- stack: float32 [8, 128, 1024], P('pix', 'chan')
Inputs may be any that keep to these rules, and one draw needn't show every extreme that they name: `owner`: within each strip column every index 0 to 3 owns between 1 and 6 blocks, some index exactly 6; -1 marks masked blocks. `stamp_block`: A listed rank is below the number of blocks that the list's index owns in the list's strip column; -1 marks an empty slot; for some shard every list fills all 2 slots.
All inputs are finite; a program needn't handle non-finite values.
Results may differ from a plain program's by a relative error of at most 0.0043.
Values may be sent and summed in bfloat16 or wider, within the bound.
A program may use at most 128 MiB of HBM per device.

v0:
```python
import functools
import math

import jax
import jax.numpy as jnp
import numpy as np
from jax import lax
from jax.experimental import pallas as pl
from jax.experimental.pallas import tpu as pltpu
from jax.sharding import PartitionSpec as P

MESH = pl.DeviceIdType.MESH
STEP = 16
LANES = 128


def trig_tables(size):
    inner = 32
    outer = size // inner
    mode = np.arange(size // 2 + 1)
    fine = 2.0 * np.pi * ((mode[None, :] * np.arange(inner)[:, None]) % size) / size
    coarse = 2.0 * np.pi * ((mode[:, None] * inner * np.arange(outer)[None, :]) % size) / size
    left = np.concatenate([np.cos(fine), -np.sin(fine)], axis=1)
    right = np.concatenate([np.cos(coarse), np.sin(coarse)], axis=0)
    return left.astype(np.float32), right.astype(np.float32)


def filter_rows(delay_gain, first, width):
    size = delay_gain.shape[0]
    half = size // 2
    zero = jnp.zeros((1,), jnp.float32)
    even = delay_gain[: half + 1]
    odd = jnp.concatenate([zero, delay_gain[half + 1 :], zero])
    inside = jnp.concatenate([zero, jnp.ones((half - 1,), jnp.float32), zero])
    gains = jnp.stack([even + odd, (even - odd) * inside]) * (1.0 / size)
    left, right = trig_tables(size)
    scaled = jnp.concatenate([gains, gains], axis=1)[:, None, :] * left[None]
    kernels = jnp.einsum(
        "hbk,ka->hab", scaled, right, precision=lax.Precision.HIGHEST, preferred_element_type=jnp.float32
    ).reshape(2, size)
    diff = jnp.roll(kernels[0], -first)
    add = jnp.roll(kernels[1], -first)
    diff_rows = jnp.stack([jnp.roll(diff, i) for i in range(8)])
    add_rows = jnp.stack([jnp.roll(add, -i) for i in range(8)])
    return diff_rows, add_rows


def compute_kernel(shards, per_shard, stamp, block_s, start_s, weight_s, diff_ref, add_ref, sky_ref, out_ref, held, filt):
    step = pl.program_id(0)
    size = diff_ref.shape[1]
    width = held.shape[1]
    here = pl.multiple_of(step * STEP, STEP)
    held[:, pl.ds(here, STEP), :] = jnp.swapaxes(sky_ref[...], 0, 1)

    @pl.when(step == pl.num_programs(0) - 1)
    def _():
        @pl.loop(0, size // 8)
        def _(t):
            diff = pltpu.roll(diff_ref[...], t * 8, 1)[:, :width]
            add = pltpu.roll(add_ref[...], size - t * 8, 1)[:, :width]
            rows = (diff + add).astype(jnp.bfloat16).astype(jnp.float32)
            for h in range(width // LANES):
                filt[h, pl.ds(pl.multiple_of(t * 8, 8), 8), :] = rows[:, h * LANES : (h + 1) * LANES]

        pixels = held.shape[2]
        tile = 256

        @pl.loop(0, shards)
        def _(q):
            for n in range(pixels // tile):
                total = jnp.zeros((stamp, tile), jnp.float32)
                for j in range(per_shard):
                    slot = q * per_shard + j
                    halves = [filt[h, pl.ds(start_s[slot], stamp), :] for h in range(width // LANES)]
                    rows = jnp.concatenate(halves, axis=1).astype(jnp.bfloat16)
                    columns = held[block_s[slot], :, n * tile : (n + 1) * tile]
                    total += weight_s[slot] * jnp.dot(rows, columns, preferred_element_type=jnp.float32)
                out_ref[q, :, n * tile : (n + 1) * tile] = total.astype(jnp.bfloat16)


def reduce_kernel(groups, shards, part_ref, out_ref, near, mid, far, send1, recv1, send2, recv2):
    k = lax.axis_index("chan")
    p = lax.axis_index("pix")
    rows = out_ref.shape[0]
    barrier = pltpu.get_barrier_semaphore()
    for e in range(1, groups):
        pl.semaphore_signal(barrier, inc=1, device_id=(lax.rem(k + e, groups), p), device_id_type=MESH)
    for d in range(1, shards):
        pl.semaphore_signal(barrier, inc=1, device_id=(k, lax.rem(p + d, shards)), device_id_type=MESH)
    pl.semaphore_wait(barrier, groups + shards - 2)

    order = list(range(1, shards)) + [0]

    def first(d, e):
        q = lax.rem(p + d, shards)
        to = lax.rem(k + e, groups)
        return pltpu.make_async_remote_copy(
            src_ref=part_ref.at[q, pl.ds(pl.multiple_of(to * rows, rows), rows)],
            dst_ref=near.at[e - 1, d],
            send_sem=send1.at[e - 1, d],
            recv_sem=recv1.at[e - 1, d],
            device_id=(to, p),
            device_id_type=MESH,
        )

    def second(d):
        return pltpu.make_async_remote_copy(
            src_ref=mid.at[d],
            dst_ref=far.at[d - 1],
            send_sem=send2.at[d],
            recv_sem=recv2.at[d],
            device_id=(k, lax.rem(p + d, shards)),
            device_id_type=MESH,
        )

    for d in order:
        for e in range(1, groups):
            first(d, e).start()
    for d in order:
        q = lax.rem(p + d, shards)
        for e in range(1, groups):
            first(d, e).wait_recv()
        total = part_ref[q, pl.ds(pl.multiple_of(k * rows, rows), rows), :].astype(jnp.float32)
        for e in range(1, groups):
            total += near[e - 1, d].astype(jnp.float32)
        if d:
            mid[d] = total.astype(jnp.bfloat16)
            second(d).start()
        else:
            out_ref[...] = total
    for d in range(1, shards):
        second(d).wait_recv()
        out_ref[...] += far[d - 1].astype(jnp.float32)
    for d in range(1, shards):
        second(d).wait_send()
    for d in order:
        for e in range(1, groups):
            first(d, e).wait_send()


def body(sky_map, owner, stamp_block, chan_start, overdensity, delay_gain, *, groups, shards):
    k = lax.axis_index("chan")
    p = lax.axis_index("pix")
    width, blocks, pixels = sky_map.shape
    stamp = 128
    rows = stamp // groups
    slots = stamp_block.shape[3]
    per_shard = groups * slots

    lists = jnp.stack([stamp_block[0, 0], chan_start[0, 0]])
    every = [lists]
    for e in range(1, groups):
        every.append(lax.ppermute(lists, "chan", [(i, (i + e) % groups) for i in range(groups)]))
    every = jnp.stack(every, axis=2)
    index = (k - jnp.arange(groups, dtype=jnp.int32)) % groups
    ranks, starts = every[0], every[1]
    block_ids = jnp.arange(blocks, dtype=jnp.int32)
    same = owner[:, None] == owner[None, :]
    earlier = block_ids[None, :] < block_ids[:, None]
    block_rank = jnp.sum((same & earlier).astype(jnp.int32), axis=1)
    match = (owner == index[:, None, None]) & (block_rank == ranks[..., None])
    match = match & (ranks >= 0)[..., None]
    block_of = jnp.sum(jnp.where(match, block_ids, 0), axis=3)
    live = jnp.any(match, axis=3)
    by_column = lax.dynamic_index_in_dim(overdensity, p, 0, False)
    weights = jnp.take(by_column, index, axis=0).transpose(1, 0, 2)
    weights = jnp.where(live, weights, 0.0)
    diff_rows, add_rows = filter_rows(delay_gain, k * width, width)

    partial = pl.pallas_call(
        functools.partial(compute_kernel, shards, per_shard, stamp),
        out_shape=jax.ShapeDtypeStruct((shards, stamp, pixels), jnp.bfloat16),
        grid_spec=pltpu.PrefetchScalarGridSpec(
            num_scalar_prefetch=3,
            grid=(width // STEP,),
            in_specs=[
                pl.BlockSpec(diff_rows.shape, lambda i, *_: (0, 0)),
                pl.BlockSpec(add_rows.shape, lambda i, *_: (0, 0)),
                pl.BlockSpec((STEP, blocks, pixels), lambda i, *_: (i, 0, 0)),
            ],
            out_specs=pl.BlockSpec((shards, stamp, pixels), lambda i, *_: (0, 0, 0)),
            scratch_shapes=[
                pltpu.VMEM((blocks, width, pixels), jnp.bfloat16),
                pltpu.VMEM((width // LANES, delay_gain.shape[0], LANES), jnp.float32),
            ],
        ),
        compiler_params=pltpu.CompilerParams(vmem_limit_bytes=48 << 20),
        name="partial_stacks",
    )(block_of.reshape(-1), starts.reshape(-1), weights.reshape(-1), diff_rows, add_rows, sky_map)

    out = pl.pallas_call(
        functools.partial(reduce_kernel, groups, shards),
        out_shape=jax.ShapeDtypeStruct((rows, pixels), jnp.float32),
        in_specs=[pl.BlockSpec(memory_space=pltpu.VMEM)],
        out_specs=pl.BlockSpec(memory_space=pltpu.VMEM),
        scratch_shapes=[
            pltpu.VMEM((groups - 1, shards, rows, pixels), jnp.bfloat16),
            pltpu.VMEM((shards, rows, pixels), jnp.bfloat16),
            pltpu.VMEM((shards - 1, rows, pixels), jnp.bfloat16),
            pltpu.SemaphoreType.DMA((groups - 1, shards)),
            pltpu.SemaphoreType.DMA((groups - 1, shards)),
            pltpu.SemaphoreType.DMA((shards,)),
            pltpu.SemaphoreType.DMA((shards,)),
        ],
        compiler_params=pltpu.CompilerParams(collective_id=0, has_side_effects=True),
        name="reduce_stacks",
    )(partial)
    return out[None]


def solution(mesh):
    in_specs = (
        P("chan", "pix", None),
        P("pix"),
        P("pix", "chan", None, None),
        P("pix", "chan", None, None),
        P(),
        P(),
    )
    run = functools.partial(body, groups=mesh.shape["chan"], shards=mesh.shape["pix"])
    return jax.shard_map(run, mesh=mesh, in_specs=in_specs, out_specs=P("pix", "chan", None), check_vma=False)
```

profile of v0, /device:TPU:0, one launch (start us, length us, event | category | flops | bytes accessed | tf_op | source)
XLA Modules:
  0.0 83.8 jit_solution(8528551085758167961)
XLA Ops:
  0.0 0.7 fusion.11
  0.7 2.9 %collective-permute-start.1 = (s32[2,8,2]{1,2,0:T(2,128)S(1)}, s32[2,8,2]{1,2,0:T(2,128)S(1)}, u32[]{:S(2)}, u32[]{:S(2)}) collective-permute-start(s32[2,8,2]{1,2,0:T(2,128)S(1)} %get-tuple-element.13), channel_id=1, source_target_pairs={{0,16},{8,24},{16,0},{24,8},{1,17},{9,25},{17,1},{25,9},{2,18},{10... | collective-permute-start | bytes 392 | tf_op jit(solution)/shard_map/ppermute | solution.py:153
  3.7 1.7 %collective-permute-start.2 = (s32[2,8,2]{1,2,0:T(2,128)S(1)}, s32[2,8,2]{1,2,0:T(2,128)S(1)}, u32[]{:S(2)}, u32[]{:S(2)}) collective-permute-start(s32[2,8,2]{1,2,0:T(2,128)S(1)} %get-tuple-element.13), channel_id=1, source_target_pairs={{0,24},{8,0},{16,8},{24,16},{1,25},{9,1},{17,9},{25,17},{2,26},{10... | collective-permute-start | bytes 392 | tf_op jit(solution)/shard_map/ppermute | solution.py:153
  5.5 0.8 slice.135
  6.2 0.8 fusion.7
  7.0 0.1 pad_maximum_fusion
  7.1 1.4 %convolution_bitcast_fusion = f32[2,32,32]{1,2,0:T(8,128)S(1)} fusion(f32[1026,32,1]{0,1,2:T(8,128)} %constant.85, f32[32,1026]{1,0:T(8,128)} %constant.84, f32[2,1026]{1,0:T(2,128)S(1)} %pad_maximum_fusion), kind=kOutput, calls=%fused_computation.1 | convolution fusion | flops 25280640 | bytes 279056 | tf_op jit(solution)/shard_map/hbk,ka->hab/dot_general | solution.py:38
  8.5 0.1 squeeze.13
  8.7 0.1 squeeze.12
  8.8 0.1 fusion.5
  8.9 0.5 slice.153
  9.4 0.6 slice.137
  10.0 0.1 slice.149
  10.1 0.1 slice.147
  10.2 0.1 slice.145
  10.2 0.1 slice.143
  10.3 0.1 slice.141
  10.4 0.1 slice.139
  11.0 0.9 %convert_reduce_fusion = s32[32]{0:T(128)S(1)} fusion(s32[32]{0:T(128)} %param.11), kind=kLoop, calls=%fused_computation.8 | loop fusion | flops 5088 | bytes 256 | tf_op jit(solution)/shard_map/reduce_sum | solution.py:160
  11.9 0.7 broadcast_compare_fusion.1
  12.6 0.6 gather_fusion
  13.2 0.1 pad_maximum_fusion.3
  13.3 0.1 pad_maximum_fusion.4
  13.3 0.1 pad_maximum_fusion.5
  13.4 0.1 pad_maximum_fusion.6
  13.5 0.1 pad_maximum_fusion.7
  13.6 0.1 pad_maximum_fusion.8
  13.7 0.7 pad_maximum_fusion.2
  14.4 0.1 pad_maximum_fusion.15
  14.4 0.1 pad_maximum_fusion.14
  14.5 0.1 pad_maximum_fusion.13
  14.6 0.1 pad_maximum_fusion.12
  14.7 0.1 pad_maximum_fusion.11
  14.7 0.1 pad_maximum_fusion.10
  14.8 0.7 pad_maximum_fusion.9
  15.8 0.3 fusion.3
  16.1 0.3 select_reduce_fusion
  16.4 0.1 bitcast_select_fusion
  16.4 0.1 copy.31
  16.6 0.1 reshape.124.weight_s
  16.7 0.1 copy.27
  16.8 0.1 reshape.123.block_s
  16.9 0.1 copy.28
  17.0 0.1 reshape_squeeze.3.start_s
  17.1 32.8 %partial_stacks.1.part_ref = bf16[8,128,1024]{2,1,0:T(8,128)(2,1)S(1)} custom-call(s32[64]{0:T(128)S(1)} %reshape.123.block_s, s32[64]{0:T(128)S(1)} %reshape_squeeze.3.start_s, f32[64]{0:T(128)S(1)} %reshape.124.weight_s, f32[8,1024]{1,0:T(8,128)S(1)} %stack.98.diff_ref, f32[8,1024]{1,0:T(8,128)S(1)} %stack.107.add_ref, bf16[256,32,1024]{2,1,0:T(8,128)(2,1)} %sky_ref.1), custom_call_target="tpu_custom_call" | custom-call | tf_op jit(solution)/shard_map/partial_stacks/pallas_call | solution.py:170
  50.0 1.3 %copy-done.1 = bf16[8,128,1024]{2,1,0:T(8,128)(2,1)} copy-done((bf16[8,128,1024]{2,1,0:T(8,128)(2,1)}, bf16[8,128,1024]{2,1,0:T(8,128)(2,1)S(1)}, u32[]{:S(2)}) %copy-start.1) | copy-done | bytes 2097176
  51.3 30.9 %reduce_stacks.1 = f32[32,1024]{1,0:T(8,128)} custom-call(bf16[8,128,1024]{2,1,0:T(8,128)(2,1)} %copy-done.1), custom_call_target="tpu_custom_call" | custom-call | tf_op jit(solution)/shard_map/reduce_stacks/pallas_call | solution.py:191
  82.2 1.6 %copy.40 = f32[1,32,1024]{2,1,0:T(8,128)} copy(f32[1,32,1024]{2,1,0:T(8,128)} %bitcast.46) | data formatting | bytes 262144
  (39 shorter events, 0.9 us)
Async XLA Ops:
  0.0 12.6 %copy-start = (f32[8,4,8,2]{2,3,1,0:T(2,128)S(1)}, f32[8,4,8,2]{2,3,1,0:T(2,128)}, u32[]{:S(2)}) copy-start(f32[8,4,8,2]{2,3,1,0:T(2,128)} %param.14) | copy-start | bytes 6148
  0.7 14.9 %collective-permute-start.1 = (s32[2,8,2]{1,2,0:T(2,128)S(1)}, s32[2,8,2]{1,2,0:T(2,128)S(1)}, u32[]{:S(2)}, u32[]{:S(2)}) collective-permute-start(s32[2,8,2]{1,2,0:T(2,128)S(1)} %get-tuple-element.13), channel_id=1, source_target_pairs={{0,16},{8,24},{16,0},{24,8},{1,17},{9,25},{17,1},{25,9},{2,18},{10... | collective-permute-start | bytes 392 | tf_op jit(solution)/shard_map/ppermute | solution.py:153
  3.6 12.0 %collective-permute-start = (s32[2,8,2]{1,2,0:T(2,128)S(1)}, s32[2,8,2]{1,2,0:T(2,128)S(1)}, u32[]{:S(2)}, u32[]{:S(2)}) collective-permute-start(s32[2,8,2]{1,2,0:T(2,128)S(1)} %get-tuple-element.13), channel_id=1, source_target_pairs={{0,8},{8,16},{16,24},{24,0},{1,9},{9,17},{17,25},{25,1},{2,10},{10... | collective-permute-start | bytes 392 | tf_op jit(solution)/shard_map/ppermute | solution.py:153
  3.7 12.0 %collective-permute-start.2 = (s32[2,8,2]{1,2,0:T(2,128)S(1)}, s32[2,8,2]{1,2,0:T(2,128)S(1)}, u32[]{:S(2)}, u32[]{:S(2)}) collective-permute-start(s32[2,8,2]{1,2,0:T(2,128)S(1)} %get-tuple-element.13), channel_id=1, source_target_pairs={{0,24},{8,0},{16,8},{24,16},{1,25},{9,1},{17,9},{25,17},{2,26},{10... | collective-permute-start | bytes 392 | tf_op jit(solution)/shard_map/ppermute | solution.py:153
  50.0 1.3 %copy-start.1 = (bf16[8,128,1024]{2,1,0:T(8,128)(2,1)}, bf16[8,128,1024]{2,1,0:T(8,128)(2,1)S(1)}, u32[]{:S(2)}) copy-start(bf16[8,128,1024]{2,1,0:T(8,128)(2,1)S(1)} %partial_stacks.1.part_ref) | copy-start | bytes 6291460
where the time goes:
time: 84.4 us; the launch traced here: 83.8 us
  Pallas kernels  63.7 us (75%)
  local copies, waits for them, and re-layouts  7.43 us (9%)
  other arithmetic  6.36 us (8%)
  starting transfers between devices  4.68 us (6%)
  matrix products  1.35 us (2%)
    pallas_call x1, Pallas kernels, body(): pl.pallas_call(functools.partial(compute_kernel, shards, per_shard, stamp...  32.8 us
    pallas_call x1, Pallas kernels, body(): pl.pallas_call(functools.partial(reduce_kernel, groups, shards), out_shap...  30.9 us
    ppermute x3, starting transfers between devices, body(): lax.ppermute(lists, 'chan', [(i, (i + e) % groups) for i in range(groups)])  4.68 us
    unnamed x5, local copies, waits for them, and re-layouts  2.91 us
  transfers between devices with their start and end apart: 3, of which 0 were waited for; matrix products, arithmetic and copies ran while one was open for 12% of the time, Pallas kernels for 0%

commit v1 on v0

v1 whole, which is shorter than its diff:
```python
import functools

import jax
import jax.numpy as jnp
import numpy as np
from jax import lax
from jax.experimental import pallas as pl
from jax.experimental.pallas import tpu as pltpu
from jax.sharding import PartitionSpec as P

MESH = pl.DeviceIdType.MESH
STEP = 32
LANES = 128


def filter_kernels(delay_gain):
    size = delay_gain.shape[0]
    half = size // 2
    mode = np.arange(half + 1)[:, None]
    angle = 2.0 * np.pi * ((mode * np.arange(size)[None, :]) % size) / size
    table = (np.cos(angle) / size).astype(np.float32)
    even = delay_gain[: half + 1]
    odd = jnp.pad(delay_gain[half + 1 :], (1, 1))
    mode = jnp.arange(half + 1, dtype=jnp.int32)
    inside = (mode > 0) & (mode < half)
    gains = jnp.stack([even + odd, jnp.where(inside, even - odd, 0.0)])
    return jnp.dot(gains, table, precision=lax.Precision.HIGHEST, preferred_element_type=jnp.float32)


def resolve_slots(groups, shards, slots, k, owner_s, lists_s, over_s, table, count, block_s, start_s, weight_s):
    blocks = owner_s.shape[0]
    for c in range(groups):
        count[c] = 0

    @pl.loop(0, blocks)
    def _(b):
        c = owner_s[b]

        @pl.when(c >= 0)
        def _():
            table[c * blocks + count[c]] = b
            count[c] = count[c] + 1

    for e in range(groups):
        c = lax.rem(k + groups - e, groups)

        @pl.loop(0, shards)
        def _(q):
            for s in range(slots):
                at = q * slots + s
                rank = lists_s[2 * e * shards * slots + at]
                live = (rank >= 0) & (rank < count[c])
                safe = jnp.where(live, rank, 0)
                to = (q * groups + e) * slots + s
                block_s[to] = jnp.where(live, table[c * blocks + safe], 0)
                start_s[to] = lists_s[(2 * e + 1) * shards * slots + at]
                weight_s[to] = jnp.where(live, over_s[c * shards * slots + at], 0.0)


def fill_filter(first, kernels_ref, filt):
    size = kernels_ref.shape[1]
    halves = filt.shape[0]
    row = lax.broadcasted_iota(jnp.int32, (8, size), 0)
    back = lax.rem(size - first, size)
    diff = pltpu.roll(jnp.broadcast_to(kernels_ref[0:1, :], (8, size)), back, 1)
    add = pltpu.roll(jnp.broadcast_to(kernels_ref[1:2, :], (8, size)), back, 1)
    diff_rows, add_rows = diff, add
    for i in range(1, 8):
        diff_rows = jnp.where(row == i, pltpu.roll(diff, i, 1), diff_rows)
        add_rows = jnp.where(row == i, pltpu.roll(add, size - i, 1), add_rows)
    lanes = size // LANES
    for v in range(LANES // 8):
        right = pltpu.roll(diff_rows, 8 * v, 1) if v else diff_rows
        left = pltpu.roll(add_rows, size - 8 * v, 1) if v else add_rows
        for u in range(lanes):
            for h in range(halves):
                a = (h - u) % lanes
                b = (h + u) % lanes
                rows = right[:, a * LANES : (a + 1) * LANES] + left[:, b * LANES : (b + 1) * LANES]
                rows = rows.astype(jnp.bfloat16).astype(jnp.float32)
                filt[h, u * LANES + 8 * v : u * LANES + 8 * v + 8, :] = rows


def compute_kernel(
    groups, shards, slots, stamp, owner_s, lists_s, over_s, kernels_ref, sky_ref, out_ref, held, filt, table, count,
    block_s, start_s, weight_s,
):
    step = pl.program_id(0)
    width = held.shape[1]
    per_shard = groups * slots
    k = lax.axis_index("chan")

    @pl.when(step == 0)
    def _():
        resolve_slots(groups, shards, slots, k, owner_s, lists_s, over_s, table, count, block_s, start_s, weight_s)
        fill_filter(k * width, kernels_ref, filt)

    for i in range(sky_ref.shape[0] // 16):
        here = pl.multiple_of(step * sky_ref.shape[0] + 16 * i, 16)
        held[:, pl.ds(here, 16), :] = jnp.swapaxes(sky_ref[16 * i : 16 * i + 16], 0, 1)

    @pl.when(step == pl.num_programs(0) - 1)
    def _():
        pixels = held.shape[2]
        tile = 256

        @pl.loop(0, shards)
        def _(q):
            for n in range(pixels // tile):
                total = jnp.zeros((stamp, tile), jnp.float32)
                for j in range(per_shard):
                    slot = q * per_shard + j
                    parts = [filt[h, pl.ds(start_s[slot], stamp), :] for h in range(width // LANES)]
                    rows = jnp.concatenate(parts, axis=1).astype(jnp.bfloat16)
                    columns = held[block_s[slot], :, n * tile : (n + 1) * tile]
                    total += weight_s[slot] * jnp.dot(rows, columns, preferred_element_type=jnp.float32)
                out_ref[q, :, n * tile : (n + 1) * tile] = total.astype(jnp.bfloat16)


def reduce_kernel(
    chips, shards, part_ref, out_ref, pair, mid1, near, keep, mid2, far, send0, recv0, send1, recv1, send2, recv2
):
    k = lax.axis_index("chan")
    p = lax.axis_index("pix")
    x = k // 2
    core = lax.rem(k, 2)
    other = 1 - core
    barrier = pltpu.get_barrier_semaphore()
    pl.semaphore_signal(barrier, inc=1, device_id=(x * 2 + other, p), device_id_type=MESH)
    for j in range(1, chips):
        pl.semaphore_signal(barrier, inc=1, device_id=(lax.rem(x + j, chips) * 2 + core, p), device_id_type=MESH)
    for d in range(1, shards):
        pl.semaphore_signal(barrier, inc=1, device_id=(k, lax.rem(p + d, shards)), device_id_type=MESH)
    pl.semaphore_wait(barrier, chips + shards - 1)

    def to_core(d):
        return pltpu.make_async_remote_copy(
            src_ref=part_ref.at[lax.rem(p + d, shards), :, other],
            dst_ref=pair.at[d],
            send_sem=send0.at[d],
            recv_sem=recv0.at[d],
            device_id=(x * 2 + other, p),
            device_id_type=MESH,
        )

    def to_chip(d, j):
        return pltpu.make_async_remote_copy(
            src_ref=mid1.at[d, j - 1],
            dst_ref=near.at[d, j - 1],
            send_sem=send1.at[d, j - 1],
            recv_sem=recv1.at[d, j - 1],
            device_id=(lax.rem(x + j, chips) * 2 + core, p),
            device_id_type=MESH,
        )

    def to_shard(d):
        return pltpu.make_async_remote_copy(
            src_ref=mid2.at[d],
            dst_ref=far.at[d - 1],
            send_sem=send2.at[d],
            recv_sem=recv2.at[d],
            device_id=(k, lax.rem(p + d, shards)),
            device_id_type=MESH,
        )

    def pair_sum(d, j):
        to = lax.rem(x + j, chips)
        mine = part_ref[lax.rem(p + d, shards), to, core].astype(jnp.float32)
        return mine + pair[d, to].astype(jnp.float32)

    def chip_stage(d):
        to_core(d).wait_recv()
        for j in range(1, chips):
            mid1[d, j - 1] = pair_sum(d, j).astype(jnp.bfloat16)
            to_chip(d, j).start()
        keep[d] = pair_sum(d, 0)

    def shard_stage(d):
        total = keep[d]
        for j in range(1, chips):
            to_chip(d, j).wait_recv()
            total += near[d, j - 1].astype(jnp.float32)
        if d:
            mid2[d] = total.astype(jnp.bfloat16)
            to_shard(d).start()
        else:
            out_ref[...] = total

    order = list(range(1, shards)) + [0]
    for d in order:
        to_core(d).start()
    lag = 2
    for i in range(shards + lag):
        if i < shards:
            chip_stage(order[i])
        if i >= lag:
            shard_stage(order[i - lag])
    for d in range(1, shards):
        to_shard(d).wait_recv()
        out_ref[...] += far[d - 1].astype(jnp.float32)
    for d in range(shards):
        to_core(d).wait_send()
        for j in range(1, chips):
            to_chip(d, j).wait_send()
        if d:
            to_shard(d).wait_send()


def body(sky_map, owner, stamp_block, chan_start, overdensity, delay_gain, *, groups, shards):
    p = lax.axis_index("pix")
    width, blocks, pixels = sky_map.shape
    stamp = 128
    chips = groups // 2
    rows = stamp // groups
    slots = stamp_block.shape[3]
    per_column = groups * shards * slots

    lists = jnp.concatenate([stamp_block.reshape(-1), chan_start.reshape(-1)])
    every = [lists]
    for e in range(1, groups):
        every.append(lax.ppermute(lists, "chan", [(i, (i + e) % groups) for i in range(groups)]))
    every = jnp.concatenate(every)
    by_column = lax.dynamic_index_in_dim(overdensity, p, 0, False).reshape(-1)
    kernels = filter_kernels(delay_gain)
    step = min(STEP, width)

    partial = pl.pallas_call(
        functools.partial(compute_kernel, groups, shards, slots, stamp),
        out_shape=jax.ShapeDtypeStruct((shards, stamp, pixels), jnp.bfloat16),
        grid_spec=pltpu.PrefetchScalarGridSpec(
            num_scalar_prefetch=3,
            grid=(width // step,),
            in_specs=[
                pl.BlockSpec(kernels.shape, lambda i, *_: (0, 0)),
                pl.BlockSpec((step, blocks, pixels), lambda i, *_: (i, 0, 0)),
            ],
            out_specs=pl.BlockSpec((shards, stamp, pixels), lambda i, *_: (0, 0, 0)),
            scratch_shapes=[
                pltpu.VMEM((blocks, width, pixels), jnp.bfloat16),
                pltpu.VMEM((width // LANES, delay_gain.shape[0], LANES), jnp.float32),
                pltpu.SMEM((groups * blocks,), jnp.int32),
                pltpu.SMEM((groups,), jnp.int32),
                pltpu.SMEM((per_column,), jnp.int32),
                pltpu.SMEM((per_column,), jnp.int32),
                pltpu.SMEM((per_column,), jnp.float32),
            ],
        ),
        compiler_params=pltpu.CompilerParams(vmem_limit_bytes=48 << 20),
        name="partial_stacks",
    )(owner, every, by_column, kernels, sky_map)

    dma = pltpu.SemaphoreType.DMA
    out = pl.pallas_call(
        functools.partial(reduce_kernel, chips, shards),
        out_shape=jax.ShapeDtypeStruct((rows, pixels), jnp.float32),
        in_specs=[pl.BlockSpec(memory_space=pltpu.VMEM)],
        out_specs=pl.BlockSpec(memory_space=pltpu.VMEM),
        scratch_shapes=[
            pltpu.VMEM((shards, chips, rows, pixels), jnp.bfloat16),
            pltpu.VMEM((shards, chips - 1, rows, pixels), jnp.bfloat16),
            pltpu.VMEM((shards, chips - 1, rows, pixels), jnp.bfloat16),
            pltpu.VMEM((shards, rows, pixels), jnp.float32),
            pltpu.VMEM((shards, rows, pixels), jnp.bfloat16),
            pltpu.VMEM((shards - 1, rows, pixels), jnp.bfloat16),
            dma((shards,)),
            dma((shards,)),
            dma((shards, chips - 1)),
            dma((shards, chips - 1)),
            dma((shards,)),
            dma((shards,)),
        ],
        compiler_params=pltpu.CompilerParams(collective_id=0, has_side_effects=True),
        name="reduce_stacks",
    )(partial.reshape(shards, chips, 2, rows, pixels))
    return out[None]


def solution(mesh):
    in_specs = (
        P("chan", "pix", None),
        P("pix"),
        P("pix", "chan", None, None),
        P("pix", "chan", None, None),
        P(),
        P(),
    )
    run = functools.partial(body, groups=mesh.shape["chan"], shards=mesh.shape["pix"])
    return jax.shard_map(run, mesh=mesh, in_specs=in_specs, out_specs=P("pix", "chan", None), check_vma=False)
```

time: 84.4 us -> 56.3 us (0.67)
  Pallas kernels: 63.7 us -> 43.4 us
  other arithmetic: 6.36 us -> 0.84 us
  local copies, waits for them, and re-layouts: 7.43 us -> 5.66 us
  starting transfers between devices: 4.68 us -> 3.17 us
  matrix products: 1.35 us -> 2.77 us
    pallas_call x2, Pallas kernels: 63.7 us -> 43.4 us  [the longest x1 24.5 us: body(): pl.pallas_call(functools.partial(reduce_kernel, chips, shards), out_shape...]
    concatenate x16 -> x1, other arithmetic: 2.48 us -> 0.08 us  [body(): lists = jnp.concatenate([stamp_block.reshape(-1), chan_start.reshape(-1)])]
    slice x28 -> x1, local copies, waits for them, and re-layouts: 3.09 us -> 0.76 us  [filter_kernels(): odd = jnp.pad(delay_gain[half + 1:], (1, 1))]
    unnamed x5 -> x9, local copies, waits for them, and re-layouts: 2.91 us -> 4.44 us
    ppermute x3, starting transfers between devices: 4.68 us -> 3.17 us  [body(): lax.ppermute(lists, 'chan', [(i, (i + e) % groups) for i in range(groups)])]
    dot_general x1, matrix products: 1.35 us -> 2.77 us  [filter_kernels(): jnp.dot(gains, table, precision=lax.Precision.HIGHEST, preferred_element_...]
    reduce_sum x2 -> x0, other arithmetic: 1.21 us -> none  [the longest x1 0.91 us: body(): block_rank = jnp.sum((same & earlier).astype(jnp.int32), axis=1)]
  transfers between devices with their start and end apart: 3 -> 3, of which waited for: 0 -> 0; matrix products, arithmetic and copies ran while one was open for 12% -> 8% of each run, Pallas kernels for 0% -> 0%
where the time goes in v1:
time: 56.3 us; the launch traced here: 55.9 us
  Pallas kernels  43.4 us (77%)
  local copies, waits for them, and re-layouts  5.66 us (10%)
  starting transfers between devices  3.17 us (6%)
  matrix products  2.77 us (5%)
  other arithmetic  0.84 us (1%)
    pallas_call x1, Pallas kernels, body(): pl.pallas_call(functools.partial(reduce_kernel, chips, shards), out_shape...  24.5 us
    pallas_call x1, Pallas kernels, body(): pl.pallas_call(functools.partial(compute_kernel, groups, shards, slots, s...  18.8 us
    unnamed x9, local copies, waits for them, and re-layouts  4.44 us
    ppermute x3, starting transfers between devices, body(): lax.ppermute(lists, 'chan', [(i, (i + e) % groups) for i in range(groups)])  3.17 us
    dot_general x1, matrix products, filter_kernels(): jnp.dot(gains, table, precision=lax.Precision.HIGHEST, preferred_element_...  2.77 us
  transfers between devices with their start and end apart: 3, of which 0 were waited for; matrix products, arithmetic and copies ran while one was open for 8% of the time, Pallas kernels for 0%

profile of v1, /device:TPU:0, one launch (start us, length us, event | category | flops | bytes accessed | tf_op | source)
XLA Modules:
  0.0 55.9 jit_solution(281671702866424889)
XLA Ops:
  0.0 0.0 copy-start
  0.0 0.0 copy-start.2
  0.0 0.8 %copy.11 = s32[1,1,8,2]{3,2,1,0:T(8,128)S(1)} copy(s32[1,1,8,2]{2,3,1,0:T(2,128)} %param.9) | data formatting | bytes 128 | tf_op args[2]
  0.8 0.1 reshape.13
  0.8 0.8 %copy.12 = s32[1,1,8,2]{3,2,1,0:T(8,128)S(1)} copy(s32[1,1,8,2]{2,3,1,0:T(2,128)} %param.10) | data formatting | bytes 128 | tf_op args[3]
  1.6 0.1 reshape.14
  1.7 0.1 pad_add_fusion.1
  1.8 2.4 %collective-permute-start.2 = (s32[32]{0:T(128)S(1)}, s32[32]{0:T(128)S(1)}, u32[]{:S(2)}, u32[]{:S(2)}) collective-permute-start(s32[32]{0:T(128)S(1)} %pad_add_fusion.1), channel_id=1, source_target_pairs={{0,24},{8,0},{16,8},{24,16},{1,25},{9,1},{17,9},{25,17},{2,26},{10... | collective-permute-start | bytes 392 | tf_op jit(solution)/shard_map/ppermute | solution.py:221
  4.1 0.6 %collective-permute-start.1 = (s32[32]{0:T(128)S(1)}, s32[32]{0:T(128)S(1)}, u32[]{:S(2)}, u32[]{:S(2)}) collective-permute-start(s32[32]{0:T(128)S(1)} %pad_add_fusion.1), channel_id=1, source_target_pairs={{0,16},{8,24},{16,0},{24,8},{1,17},{9,25},{17,1},{25,9},{2,18},{10... | collective-permute-start | bytes 392 | tf_op jit(solution)/shard_map/ppermute | solution.py:221
  4.8 0.2 collective-permute-start
  4.9 0.8 %slice.7 = f32[511]{0:T(512)S(1)} slice(f32[1024]{0:T(1024)} %param.12), slice={[513:1024]} | slice | bytes 4088 | tf_op jit(solution)/shard_map/slice | solution.py:23
  5.7 0.8 %pad_add_fusion = (f32[513]{0:T(1024)S(1)}, f32[513]{0:T(1024)S(1)}) fusion(f32[511]{0:T(512)S(1)} %slice.7, f32[1024]{0:T(1024)} %param.12), kind=kLoop, calls=%fused_computation.5 | loop fusion | flops 3078 | bytes 8200 | tf_op jit(solution)/shard_map/add | solution.py:26
  6.5 0.0 copy-done
  6.5 2.8 %fusion.kernels_ref = f32[2,1024]{1,0:T(2,128)S(1)} fusion(f32[513,1024]{1,0:T(8,128)} %constant.19.clone, f32[1,513]{1,0:T(1,128)S(1)} %stack.10, f32[1,513]{1,0:T(1,128)S(1)} %stack.9), kind=kOutput, calls=%fused_computation.3 | convolution fusion | flops 12608514 | bytes 2113544 | tf_op jit(solution)/shard_map/dot_general | solution.py:27
  9.3 0.1 copy.13
  9.3 0.1 reshape.15.over_s
  9.5 0.0 collective-permute-done.2
  9.5 0.0 collective-permute-done.1
  9.5 0.0 collective-permute-done
  9.5 0.1 concatenate.8.lists_s
  9.6 0.0 copy-done.2
  9.6 18.8 %partial_stacks.1 = bf16[8,128,1024]{2,1,0:T(8,128)(2,1)S(1)} custom-call(s32[32]{0:T(128)S(1)} %copy-done.2, s32[128]{0:T(128)S(1)} %concatenate.8.lists_s, f32[64]{0:T(128)S(1)} %reshape.15.over_s, f32[2,1024]{1,0:T(2,128)S(1)} %fusion.kernels_ref, bf16[256,32,1024]{2,1,0:T(8,128)(2,1)} %sky_ref.1), custom_call_target="tpu_custom_call" | custom-call | tf_op jit(solution)/shard_map/partial_stacks/pallas_call | solution.py:227
  28.4 0.0 copy-start.1
  28.4 1.3 %copy-done.1 = bf16[8,128,1024]{2,1,0:T(8,128)(2,1)} copy-done((bf16[8,128,1024]{2,1,0:T(8,128)(2,1)}, bf16[8,128,1024]{2,1,0:T(8,128)(2,1)S(1)}, u32[]{:S(2)}) %copy-start.1) | copy-done | bytes 2097176
  29.8 24.5 %reduce_stacks.1 = f32[32,1024]{1,0:T(8,128)} custom-call(bf16[8,2,2,32,1024]{4,3,2,1,0:T(8,128)(2,1)} %bitcast.9), custom_call_target="tpu_custom_call" | custom-call | tf_op jit(solution)/shard_map/reduce_stacks/pallas_call | solution.py:253
  54.3 1.6 %copy.15 = f32[1,32,1024]{2,1,0:T(8,128)} copy(f32[1,32,1024]{2,1,0:T(8,128)} %bitcast.10) | data formatting | bytes 262144
  (3 shorter events, 0.0 us)
Async XLA Ops:
  0.0 6.5 %copy-start = (f32[8,4,8,2]{2,3,1,0:T(2,128)S(1)}, f32[8,4,8,2]{2,3,1,0:T(2,128)}, u32[]{:S(2)}) copy-start(f32[8,4,8,2]{2,3,1,0:T(2,128)} %param.11) | copy-start | bytes 6148
  0.0 9.6 %copy-start.2 = (s32[32]{0:T(128)S(1)}, s32[32]{0:T(128)}, u32[]{:S(2)}) copy-start(s32[32]{0:T(128)} %owner_s.1) | copy-start | bytes 388
  1.8 7.7 %collective-permute-start.2 = (s32[32]{0:T(128)S(1)}, s32[32]{0:T(128)S(1)}, u32[]{:S(2)}, u32[]{:S(2)}) collective-permute-start(s32[32]{0:T(128)S(1)} %pad_add_fusion.1), channel_id=1, source_target_pairs={{0,24},{8,0},{16,8},{24,16},{1,25},{9,1},{17,9},{25,17},{2,26},{10... | collective-permute-start | bytes 392 | tf_op jit(solution)/shard_map/ppermute | solution.py:221
  4.1 5.3 %collective-permute-start.1 = (s32[32]{0:T(128)S(1)}, s32[32]{0:T(128)S(1)}, u32[]{:S(2)}, u32[]{:S(2)}) collective-permute-start(s32[32]{0:T(128)S(1)} %pad_add_fusion.1), channel_id=1, source_target_pairs={{0,16},{8,24},{16,0},{24,8},{1,17},{9,25},{17,1},{25,9},{2,18},{10... | collective-permute-start | bytes 392 | tf_op jit(solution)/shard_map/ppermute | solution.py:221
  4.8 4.7 %collective-permute-start = (s32[32]{0:T(128)S(1)}, s32[32]{0:T(128)S(1)}, u32[]{:S(2)}, u32[]{:S(2)}) collective-permute-start(s32[32]{0:T(128)S(1)} %pad_add_fusion.1), channel_id=1, source_target_pairs={{0,8},{8,16},{16,24},{24,0},{1,9},{9,17},{17,25},{25,1},{2,10},{10... | collective-permute-start | bytes 392 | tf_op jit(solution)/shard_map/ppermute | solution.py:221
  28.4 1.4 %copy-start.1 = (bf16[8,128,1024]{2,1,0:T(8,128)(2,1)}, bf16[8,128,1024]{2,1,0:T(8,128)(2,1)S(1)}, u32[]{:S(2)}) copy-start(bf16[8,128,1024]{2,1,0:T(8,128)(2,1)S(1)} %partial_stacks.1) | copy-start | bytes 6291460

commit v2 on v1

v2 whole, which is shorter than its diff:
```python
import functools

import jax
import jax.numpy as jnp
import numpy as np
from jax import lax
from jax.experimental import pallas as pl
from jax.experimental.pallas import tpu as pltpu
from jax.sharding import PartitionSpec as P

MESH = pl.DeviceIdType.MESH
STEP = 32
LANES = 128
LAG1 = 2
LAG2 = 4


def filter_kernels(delay_gain):
    size = delay_gain.shape[0]
    half = size // 2
    mode = np.arange(half + 1)[:, None]
    angle = 2.0 * np.pi * ((mode * np.arange(size)[None, :]) % size) / size
    table = (np.cos(angle) / size).astype(np.float32)
    even = delay_gain[: half + 1]
    odd = jnp.pad(delay_gain[half + 1 :], (1, 1))
    mode = jnp.arange(half + 1, dtype=jnp.int32)
    inside = (mode > 0) & (mode < half)
    gains = jnp.stack([even + odd, jnp.where(inside, even - odd, 0.0)])
    return jnp.dot(gains, table, precision=lax.Precision.HIGHEST, preferred_element_type=jnp.float32)


def resolve_kernel(owner_s, ranks_s, starts_s, out_s, table):
    c = lax.axis_index("chan")
    shards, slots = ranks_s.shape

    def fill(b, count):
        table[count] = b
        return count + (owner_s[b] == c).astype(jnp.int32)

    count = lax.fori_loop(0, owner_s.shape[0], fill, jnp.int32(0))
    for q in range(shards):
        for s in range(slots):
            rank = ranks_s[q, s]
            live = (rank >= 0) & (rank < count)
            out_s[q * slots + s] = jnp.where(live, table[jnp.where(live, rank, 0)], -1)
            out_s[(shards + q) * slots + s] = starts_s[q, s]


def fill_filter(first, kernels_ref, filt):
    size = kernels_ref.shape[1]
    halves = filt.shape[0]
    row = lax.broadcasted_iota(jnp.int32, (8, size), 0)
    back = lax.rem(size - first, size)
    diff = pltpu.roll(jnp.broadcast_to(kernels_ref[0:1, :], (8, size)), back, 1)
    add = pltpu.roll(jnp.broadcast_to(kernels_ref[1:2, :], (8, size)), back, 1)
    diff_rows, add_rows = diff, add
    for i in range(1, 8):
        diff_rows = jnp.where(row == i, pltpu.roll(diff, i, 1), diff_rows)
        add_rows = jnp.where(row == i, pltpu.roll(add, size - i, 1), add_rows)
    lanes = size // LANES
    for v in range(LANES // 8):
        right = pltpu.roll(diff_rows, 8 * v, 1) if v else diff_rows
        left = pltpu.roll(add_rows, size - 8 * v, 1) if v else add_rows
        for u in range(lanes):
            for h in range(halves):
                a = (h - u) % lanes
                b = (h + u) % lanes
                rows = right[:, a * LANES : (a + 1) * LANES] + left[:, b * LANES : (b + 1) * LANES]
                rows = rows.astype(jnp.bfloat16).astype(jnp.float32)
                filt[h, u * LANES + 8 * v : u * LANES + 8 * v + 8, :] = rows


def stack_kernel(
    groups, shards, slots, stamp, lists_s, over_s, kernels_ref, sky_a, sky_b, out_ref,
    held, filt, part, pair, mid1, near, keep, mid2, far, send0, recv0, send1, recv1, send2, recv2,
):
    step = pl.program_id(0)
    width, pixels = held.shape[1:]
    chips = groups // 2
    rows = stamp // groups
    column = shards * slots
    k = lax.axis_index("chan")
    p = lax.axis_index("pix")
    x = k // 2
    core = lax.rem(k, 2)
    other = 1 - core

    @pl.when(step == 0)
    def _():
        barrier = pltpu.get_barrier_semaphore()
        pl.semaphore_signal(barrier, inc=1, device_id=(x * 2 + other, p), device_id_type=MESH)
        for j in range(1, chips):
            pl.semaphore_signal(barrier, inc=1, device_id=(lax.rem(x + j, chips) * 2 + core, p), device_id_type=MESH)
        for d in range(1, shards):
            pl.semaphore_signal(barrier, inc=1, device_id=(k, lax.rem(p + d, shards)), device_id_type=MESH)
        fill_filter(k * width, kernels_ref, filt)
        pl.semaphore_wait(barrier, chips + shards - 1)

    half = sky_a.shape[1]
    for i in range(sky_a.shape[0] // 16):
        here = pl.multiple_of(step * sky_a.shape[0] + 16 * i, 16)
        held[:half, pl.ds(here, 16), :] = jnp.swapaxes(sky_a[16 * i : 16 * i + 16], 0, 1)
        held[half:, pl.ds(here, 16), :] = jnp.swapaxes(sky_b[16 * i : 16 * i + 16], 0, 1)

    def to_core(i):
        return pltpu.make_async_remote_copy(
            src_ref=part.at[i, :, other],
            dst_ref=pair.at[i],
            send_sem=send0.at[i],
            recv_sem=recv0.at[i],
            device_id=(x * 2 + other, p),
            device_id_type=MESH,
        )

    def to_chip(i, j):
        return pltpu.make_async_remote_copy(
            src_ref=mid1.at[i, j - 1],
            dst_ref=near.at[i, j - 1],
            send_sem=send1.at[i, j - 1],
            recv_sem=recv1.at[i, j - 1],
            device_id=(lax.rem(x + j, chips) * 2 + core, p),
            device_id_type=MESH,
        )

    def to_shard(i):
        return pltpu.make_async_remote_copy(
            src_ref=mid2.at[i],
            dst_ref=far.at[i],
            send_sem=send2.at[i],
            recv_sem=recv2.at[i],
            device_id=(k, lax.rem(p + 1 + i, shards)),
            device_id_type=MESH,
        )

    def compute(i):
        q = lax.rem(p + 1 + i, shards)
        tile = 256
        for n in range(pixels // tile):
            total = jnp.zeros((stamp, tile), jnp.float32)
            for e in range(groups):
                c = lax.rem(k + groups - e, groups)
                for s in range(slots):
                    at = q * slots + s
                    block = lists_s[2 * e * column + at]
                    first = lists_s[(2 * e + 1) * column + at]
                    weight = jnp.where(block >= 0, over_s[c * column + at], 0.0)
                    parts = [filt[h, pl.ds(first, stamp), :] for h in range(width // LANES)]
                    cut = jnp.concatenate(parts, axis=1).astype(jnp.bfloat16)
                    columns = held[jnp.maximum(block, 0), :, n * tile : (n + 1) * tile]
                    total += weight * jnp.dot(cut, columns, preferred_element_type=jnp.float32)
            total = total.astype(jnp.bfloat16).reshape(chips, 2, rows, tile)
            part[i, :, :, :, n * tile : (n + 1) * tile] = total

    def pair_sum(i, j):
        to = lax.rem(x + j, chips)
        return part[i, to, core].astype(jnp.float32) + pair[i, to].astype(jnp.float32)

    def chip_stage(i):
        to_core(i).wait_recv()
        for j in range(1, chips):
            mid1[i, j - 1] = pair_sum(i, j).astype(jnp.bfloat16)
            to_chip(i, j).start()
        keep[i] = pair_sum(i, 0)

    def shard_sum(i):
        total = keep[i]
        for j in range(1, chips):
            to_chip(i, j).wait_recv()
            total += near[i, j - 1].astype(jnp.float32)
        return total

    @pl.when(step == pl.num_programs(0) - 1)
    def _():
        @pl.loop(0, shards + LAG2 - 1)
        def _(i):
            @pl.when(i < shards)
            def _():
                compute(i)
                to_core(i).start()

            @pl.when((i >= LAG1) & (i < shards + LAG1))
            def _():
                chip_stage(i - LAG1)

            @pl.when(i >= LAG2)
            def _():
                mid2[i - LAG2] = shard_sum(i - LAG2).astype(jnp.bfloat16)
                to_shard(i - LAG2).start()

        out_ref[...] = shard_sum(shards - 1)
        for i in range(shards - 1):
            to_shard(i).wait_recv()
            out_ref[...] += far[i].astype(jnp.float32)
        for i in range(shards):
            to_core(i).wait_send()
            for j in range(1, chips):
                to_chip(i, j).wait_send()
            if i < shards - 1:
                to_shard(i).wait_send()


def body(sky_map, owner, stamp_block, chan_start, overdensity, delay_gain, *, groups, shards):
    p = lax.axis_index("pix")
    width, blocks, pixels = sky_map.shape
    stamp = 128
    chips = groups // 2
    rows = stamp // groups
    slots = stamp_block.shape[3]

    smem = pl.BlockSpec(memory_space=pltpu.SMEM)
    lists = pl.pallas_call(
        resolve_kernel,
        out_shape=jax.ShapeDtypeStruct((2 * shards * slots,), jnp.int32),
        in_specs=[smem] * 3,
        out_specs=smem,
        scratch_shapes=[pltpu.SMEM((blocks + 1,), jnp.int32)],
        name="resolve_slots",
    )(owner, stamp_block[0, 0], chan_start[0, 0])
    every = [lists]
    for e in range(1, groups):
        every.append(lax.ppermute(lists, "chan", [(i, (i + e) % groups) for i in range(groups)]))
    every = jnp.concatenate(every)
    by_column = lax.dynamic_index_in_dim(overdensity, p, 0, False).reshape(-1)
    kernels = filter_kernels(delay_gain)
    step = min(STEP, width)

    dma = pltpu.SemaphoreType.DMA
    sky = (step, blocks // 2, pixels)
    out = pl.pallas_call(
        functools.partial(stack_kernel, groups, shards, slots, stamp),
        out_shape=jax.ShapeDtypeStruct((rows, pixels), jnp.float32),
        grid_spec=pltpu.PrefetchScalarGridSpec(
            num_scalar_prefetch=2,
            grid=(width // step,),
            in_specs=[
                pl.BlockSpec(kernels.shape, lambda i, *_: (0, 0)),
                pl.BlockSpec(sky, lambda i, *_: (i, 0, 0)),
                pl.BlockSpec(sky, lambda i, *_: (i, 1, 0)),
            ],
            out_specs=pl.BlockSpec((rows, pixels), lambda i, *_: (0, 0)),
            scratch_shapes=[
                pltpu.VMEM((blocks, width, pixels), jnp.bfloat16),
                pltpu.VMEM((width // LANES, delay_gain.shape[0], LANES), jnp.float32),
                pltpu.VMEM((shards, chips, 2, rows, pixels), jnp.bfloat16),
                pltpu.VMEM((shards, chips, rows, pixels), jnp.bfloat16),
                pltpu.VMEM((shards, chips - 1, rows, pixels), jnp.bfloat16),
                pltpu.VMEM((shards, chips - 1, rows, pixels), jnp.bfloat16),
                pltpu.VMEM((shards, rows, pixels), jnp.float32),
                pltpu.VMEM((shards - 1, rows, pixels), jnp.bfloat16),
                pltpu.VMEM((shards - 1, rows, pixels), jnp.bfloat16),
                dma((shards,)),
                dma((shards,)),
                dma((shards, chips - 1)),
                dma((shards, chips - 1)),
                dma((shards - 1,)),
                dma((shards - 1,)),
            ],
        ),
        compiler_params=pltpu.CompilerParams(
            collective_id=0, has_side_effects=True, vmem_limit_bytes=48 << 20
        ),
        name="stack_stamps",
    )(every, by_column, kernels, sky_map, sky_map)
    return out[None]


def solution(mesh):
    in_specs = (
        P("chan", "pix", None),
        P("pix"),
        P("pix", "chan", None, None),
        P("pix", "chan", None, None),
        P(),
        P(),
    )
    run = functools.partial(body, groups=mesh.shape["chan"], shards=mesh.shape["pix"])
    return jax.shard_map(run, mesh=mesh, in_specs=in_specs, out_specs=P("pix", "chan", None), check_vma=False)
```

time: 56.3 us -> 48.8 us (0.87)
  Pallas kernels: 43.4 us -> 37.2 us
  local copies, waits for them, and re-layouts: 5.66 us -> 4.35 us
    pallas_call x2, Pallas kernels: 43.4 us -> 37.2 us  [the longest x1 35.6 us: body(): pl.pallas_call(functools.partial(stack_kernel, groups, shards, slots, sta...]
    unnamed x9 -> x5, local copies, waits for them, and re-layouts: 4.44 us -> 0.67 us
    squeeze x0 -> x2, local copies, waits for them, and re-layouts: none -> 2.7 us  [the longest x1 1.35 us: body(): stamp_block[0, 0]]
  transfers between devices with their start and end apart: 3 -> 3, of which waited for: 0 -> 0; matrix products, arithmetic and copies ran while one was open for 8% -> 9% of each run, Pallas kernels for 0% -> 0%
where the time goes in v2:
time: 48.8 us; the launch traced here: 48.4 us
  Pallas kernels  37.2 us (76%)
  local copies, waits for them, and re-layouts  4.35 us (9%)
  starting transfers between devices  3.23 us (7%)
  matrix products  2.77 us (6%)
  other arithmetic  0.84 us (2%)
    pallas_call x1, Pallas kernels, body(): pl.pallas_call(functools.partial(stack_kernel, groups, shards, slots, sta...  35.6 us
    ppermute x3, starting transfers between devices, body(): lax.ppermute(lists, 'chan', [(i, (i + e) % groups) for i in range(groups)])  3.23 us
    dot_general x1, matrix products, filter_kernels(): jnp.dot(gains, table, precision=lax.Precision.HIGHEST, preferred_element_...  2.77 us
    pallas_call x1, Pallas kernels, body(): pl.pallas_call(resolve_kernel, out_shape=jax.ShapeDtypeStruct((2 * shards...  1.6 us
    squeeze x1, local copies, waits for them, and re-layouts, body(): stamp_block[0, 0]  1.35 us
    squeeze x1, local copies, waits for them, and re-layouts, body(): chan_start[0, 0]  1.35 us
  transfers between devices with their start and end apart: 3, of which 0 were waited for; matrix products, arithmetic and copies ran while one was open for 9% of the time, Pallas kernels for 0%

profile of v2, /device:TPU:0, one launch (start us, length us, event | category | flops | bytes accessed | tf_op | source)
XLA Modules:
  0.0 48.4 jit_solution(7769731956080357065)
XLA Ops:
  0.0 0.0 copy-start
  0.0 1.4 %copy.11.ranks_s = s32[8,2]{1,0:T(8,128)} copy(s32[8,2]{0,1:T(2,128)} %bitcast.7) | data formatting | bytes 128 | tf_op jit(solution)/shard_map/squeeze | solution.py:218
  1.4 1.3 %copy.12.starts_s = s32[8,2]{1,0:T(8,128)} copy(s32[8,2]{0,1:T(2,128)} %bitcast.8) | data formatting | bytes 128 | tf_op jit(solution)/shard_map/squeeze | solution.py:218
  2.7 1.6 %resolve_slots.1 = s32[32]{0:T(128)} custom-call(s32[32]{0:T(128)} %owner_s.1, s32[8,2]{1,0:T(8,128)} %copy.11.ranks_s, s32[8,2]{1,0:T(8,128)} %copy.12.starts_s), custom_call_target="tpu_custom_call" | custom-call | tf_op jit(solution)/shard_map/resolve_slots/pallas_call | solution.py:211
  4.3 0.0 copy-start.1
  4.3 2.4 %collective-permute-start.2 = (s32[32]{0:T(128)}, s32[32]{0:T(128)S(1)}, u32[]{:S(2)}, u32[]{:S(2)}) collective-permute-start(s32[32]{0:T(128)} %resolve_slots.1), channel_id=1, source_target_pairs={{0,24},{8,0},{16,8},{24,16},{1,25},{9,1},{17,9},{25,17},{2,26},{10... | collective-permute-start | bytes 392 | tf_op jit(solution)/shard_map/ppermute | solution.py:221
  6.8 0.6 %collective-permute-start.1 = (s32[32]{0:T(128)}, s32[32]{0:T(128)S(1)}, u32[]{:S(2)}, u32[]{:S(2)}) collective-permute-start(s32[32]{0:T(128)} %resolve_slots.1), channel_id=1, source_target_pairs={{0,16},{8,24},{16,0},{24,8},{1,17},{9,25},{17,1},{25,9},{2,18},{10... | collective-permute-start | bytes 392 | tf_op jit(solution)/shard_map/ppermute | solution.py:221
  7.4 0.2 collective-permute-start
  7.6 0.8 %slice.7 = f32[511]{0:T(512)S(1)} slice(f32[1024]{0:T(1024)} %param.12), slice={[513:1024]} | slice | bytes 4088 | tf_op jit(solution)/shard_map/slice | solution.py:25
  8.3 0.8 %pad_add_fusion = (f32[513]{0:T(1024)S(1)}, f32[513]{0:T(1024)S(1)}) fusion(f32[511]{0:T(512)S(1)} %slice.7, f32[1024]{0:T(1024)} %param.12), kind=kLoop, calls=%fused_computation.5 | loop fusion | flops 3078 | bytes 8200 | tf_op jit(solution)/shard_map/add | solution.py:28
  9.1 0.0 copy-done
  9.1 2.8 %fusion.kernels_ref = f32[2,1024]{1,0:T(2,128)S(1)} fusion(f32[513,1024]{1,0:T(8,128)} %constant.19.clone, f32[1,513]{1,0:T(1,128)S(1)} %stack.10, f32[1,513]{1,0:T(1,128)S(1)} %stack.9), kind=kOutput, calls=%fused_computation.3 | convolution fusion | flops 12608514 | bytes 2113544 | tf_op jit(solution)/shard_map/dot_general | solution.py:29
  11.9 0.1 copy.13
  12.0 0.1 reshape.4.over_s
  12.1 0.0 collective-permute-done.2
  12.1 0.0 collective-permute-done.1
  12.1 0.0 collective-permute-done
  12.1 0.0 copy-done.1
  12.1 0.1 pad_add_fusion.1.lists_s
  12.2 35.6 %stack_stamps.1 = f32[32,1024]{1,0:T(8,128)S(1)} custom-call(s32[128]{0:T(128)S(1)} %pad_add_fusion.1.lists_s, f32[64]{0:T(128)S(1)} %reshape.4.over_s, f32[2,1024]{1,0:T(2,128)S(1)} %fusion.kernels_ref, bf16[256,32,1024]{2,1,0:T(8,128)(2,1)} %sky_b.1, bf16[256,32,1024]{2,1,0:T(8,128)(2,1)} %sky_b.1), custom_call_target="tpu_custom_call" | custom-call | tf_op jit(solution)/shard_map/stack_stamps/pallas_call | solution.py:229
  47.8 0.7 %copy.15 = f32[1,32,1024]{2,1,0:T(8,128)} copy(f32[1,32,1024]{2,1,0:T(8,128)S(1)} %bitcast.6) | data formatting | bytes 262144
  (3 shorter events, 0.0 us)
Async XLA Ops:
  0.0 9.1 %copy-start = (f32[8,4,8,2]{2,3,1,0:T(2,128)S(1)}, f32[8,4,8,2]{2,3,1,0:T(2,128)}, u32[]{:S(2)}) copy-start(f32[8,4,8,2]{2,3,1,0:T(2,128)} %param.11) | copy-start | bytes 6148
  4.3 7.8 %copy-start.1 = (s32[32]{0:T(128)S(1)}, s32[32]{0:T(128)}, u32[]{:S(2)}) copy-start(s32[32]{0:T(128)} %resolve_slots.1) | copy-start | bytes 388
  4.3 7.8 %collective-permute-start.2 = (s32[32]{0:T(128)}, s32[32]{0:T(128)S(1)}, u32[]{:S(2)}, u32[]{:S(2)}) collective-permute-start(s32[32]{0:T(128)} %resolve_slots.1), channel_id=1, source_target_pairs={{0,24},{8,0},{16,8},{24,16},{1,25},{9,1},{17,9},{25,17},{2,26},{10... | collective-permute-start | bytes 392 | tf_op jit(solution)/shard_map/ppermute | solution.py:221
  6.8 5.3 %collective-permute-start.1 = (s32[32]{0:T(128)}, s32[32]{0:T(128)S(1)}, u32[]{:S(2)}, u32[]{:S(2)}) collective-permute-start(s32[32]{0:T(128)} %resolve_slots.1), channel_id=1, source_target_pairs={{0,16},{8,24},{16,0},{24,8},{1,17},{9,25},{17,1},{25,9},{2,18},{10... | collective-permute-start | bytes 392 | tf_op jit(solution)/shard_map/ppermute | solution.py:221
  7.4 4.7 %collective-permute-start = (s32[32]{0:T(128)}, s32[32]{0:T(128)S(1)}, u32[]{:S(2)}, u32[]{:S(2)}) collective-permute-start(s32[32]{0:T(128)} %resolve_slots.1), channel_id=1, source_target_pairs={{0,8},{8,16},{16,24},{24,0},{1,9},{9,17},{17,25},{25,1},{2,10},{10... | collective-permute-start | bytes 392 | tf_op jit(solution)/shard_map/ppermute | solution.py:221

commit v3 on v2

--- a/solution.py
+++ b/solution.py
@@ -15,18 +15,29 @@
 LAG2 = 4
 
 
-def filter_kernels(delay_gain):
-    size = delay_gain.shape[0]
+def cosine_table(size):
+    mode = np.arange(size // 2)[:, None]
+    angle = 2.0 * np.pi * ((mode * np.arange(size)[None, :]) % size) / size
+    return (np.cos(angle) / size).astype(np.float32)
+
+
+def filter_piece(gain_ref, table_ref, first):
+    size = gain_ref.shape[1]
     half = size // 2
-    mode = np.arange(half + 1)[:, None]
-    angle = 2.0 * np.pi * ((mode * np.arange(size)[None, :]) % size) / size
-    table = (np.cos(angle) / size).astype(np.float32)
-    even = delay_gain[: half + 1]
-    odd = jnp.pad(delay_gain[half + 1 :], (1, 1))
-    mode = jnp.arange(half + 1, dtype=jnp.int32)
-    inside = (mode > 0) & (mode < half)
-    gains = jnp.stack([even + odd, jnp.where(inside, even - odd, 0.0)])
-    return jnp.dot(gains, table, precision=lax.Precision.HIGHEST, preferred_element_type=jnp.float32)
+    piece = table_ref.shape[1]
+    gain = jnp.broadcast_to(gain_ref[...], (8, size))
+    even = gain[:, :half]
+    odd = gain[:, half:]
+    mode = lax.broadcasted_iota(jnp.int32, (8, half), 1)
+    row = lax.broadcasted_iota(jnp.int32, (8, half), 0)
+    odd = jnp.where(mode == 0, 0.0, odd)
+    minus = jnp.where(mode == 0, 0.0, even - odd)
+    gains = jnp.where(row == 0, even + odd, minus)
+    out = jnp.dot(gains, table_ref[...], precision=lax.Precision.HIGHEST, preferred_element_type=jnp.float32)
+    at = lax.broadcasted_iota(jnp.int32, (8, piece), 1) + first
+    sign = jnp.where(lax.rem(at, 2) == 0, 1.0 / size, -1.0 / size)
+    top = lax.broadcasted_iota(jnp.int32, (8, piece), 0) == 0
+    return out + jnp.where(top, gain[:, half : half + 1] * sign, 0.0)
 
 
 def resolve_kernel(owner_s, ranks_s, starts_s, out_s, table):
@@ -71,8 +82,8 @@
 
 
 def stack_kernel(
-    groups, shards, slots, stamp, lists_s, over_s, kernels_ref, sky_a, sky_b, out_ref,
-    held, filt, part, pair, mid1, near, keep, mid2, far, send0, recv0, send1, recv1, send2, recv2,
+    groups, shards, slots, stamp, over_s, lists_ref, gain_ref, table_ref, sky_a, sky_b, out_ref,
+    own_s, peers_s, peers, local, send_l, recv_l, kernels_ref, held, filt, part, pair, mid1, near, keep, mid2, far, send0, recv0, send1, recv1, send2, recv2,
 ):
     step = pl.program_id(0)
     width, pixels = held.shape[1:]
@@ -85,16 +96,37 @@
     core = lax.rem(k, 2)
     other = 1 - core
 
+    def to_peer(e):
+        return pltpu.make_async_remote_copy(
+            src_ref=lists_ref,
+            dst_ref=peers.at[pl.ds(e - 1, 1)],
+            send_sem=send_l.at[e - 1],
+            recv_sem=recv_l.at[e - 1],
+            device_id=(lax.rem(k + e, groups), p),
+            device_id_type=MESH,
+        )
+
+    own_lists = pltpu.make_async_copy(lists_ref, own_s, local.at[0])
+    peer_lists = pltpu.make_async_copy(peers, peers_s, local.at[1])
+
     @pl.when(step == 0)
     def _():
         barrier = pltpu.get_barrier_semaphore()
-        pl.semaphore_signal(barrier, inc=1, device_id=(x * 2 + other, p), device_id_type=MESH)
-        for j in range(1, chips):
-            pl.semaphore_signal(barrier, inc=1, device_id=(lax.rem(x + j, chips) * 2 + core, p), device_id_type=MESH)
+        for e in range(1, groups):
+            pl.semaphore_signal(barrier, inc=1, device_id=(lax.rem(k + e, groups), p), device_id_type=MESH)
         for d in range(1, shards):
             pl.semaphore_signal(barrier, inc=1, device_id=(k, lax.rem(p + d, shards)), device_id_type=MESH)
-        fill_filter(k * width, kernels_ref, filt)
-        pl.semaphore_wait(barrier, chips + shards - 1)
+
+    @pl.when(step == 2)
+    def _():
+        pl.semaphore_wait(pltpu.get_barrier_semaphore(), groups + shards - 2)
+        own_lists.start()
+        for e in range(1, groups):
+            to_peer(e).start()
+
+    piece = table_ref.shape[1]
+    lane = pl.multiple_of(step * piece, piece)
+    kernels_ref[:, pl.ds(lane, piece)] = filter_piece(gain_ref, table_ref, lane)
 
     half = sky_a.shape[1]
     for i in range(sky_a.shape[0] // 16):
@@ -141,8 +173,8 @@
                 c = lax.rem(k + groups - e, groups)
                 for s in range(slots):
                     at = q * slots + s
-                    block = lists_s[2 * e * column + at]
-                    first = lists_s[(2 * e + 1) * column + at]
+                    block = peers_s[e - 1, at] if e else own_s[0, at]
+                    first = peers_s[e - 1, column + at] if e else own_s[0, column + at]
                     weight = jnp.where(block >= 0, over_s[c * column + at], 0.0)
                     parts = [filt[h, pl.ds(first, stamp), :] for h in range(width // LANES)]
                     cut = jnp.concatenate(parts, axis=1).astype(jnp.bfloat16)
@@ -171,6 +203,13 @@
 
     @pl.when(step == pl.num_programs(0) - 1)
     def _():
+        for e in range(1, groups):
+            to_peer(e).wait_recv()
+        peer_lists.start()
+        fill_filter(k * width, kernels_ref, filt)
+        own_lists.wait()
+        peer_lists.wait()
+
         @pl.loop(0, shards + LAG2 - 1)
         def _(i):
             @pl.when(i < shards)
@@ -191,6 +230,8 @@
         for i in range(shards - 1):
             to_shard(i).wait_recv()
             out_ref[...] += far[i].astype(jnp.float32)
+        for e in range(1, groups):
+            to_peer(e).wait_send()
         for i in range(shards):
             to_core(i).wait_send()
             for j in range(1, chips):
@@ -210,19 +251,17 @@
     smem = pl.BlockSpec(memory_space=pltpu.SMEM)
     lists = pl.pallas_call(
         resolve_kernel,
-        out_shape=jax.ShapeDtypeStruct((2 * shards * slots,), jnp.int32),
+        out_shape=jax.ShapeDtypeStruct((LANES,), jnp.int32),
         in_specs=[smem] * 3,
         out_specs=smem,
         scratch_shapes=[pltpu.SMEM((blocks + 1,), jnp.int32)],
         name="resolve_slots",
     )(owner, stamp_block[0, 0], chan_start[0, 0])
-    every = [lists]
-    for e in range(1, groups):
-        every.append(lax.ppermute(lists, "chan", [(i, (i + e) % groups) for i in range(groups)]))
-    every = jnp.concatenate(every)
     by_column = lax.dynamic_index_in_dim(overdensity, p, 0, False).reshape(-1)
-    kernels = filter_kernels(delay_gain)
     step = min(STEP, width)
+    steps = width // step
+    size = delay_gain.shape[0]
+    piece = size // steps
 
     dma = pltpu.SemaphoreType.DMA
     sky = (step, blocks // 2, pixels)
@@ -230,17 +269,26 @@
         functools.partial(stack_kernel, groups, shards, slots, stamp),
         out_shape=jax.ShapeDtypeStruct((rows, pixels), jnp.float32),
         grid_spec=pltpu.PrefetchScalarGridSpec(
-            num_scalar_prefetch=2,
-            grid=(width // step,),
+            num_scalar_prefetch=1,
+            grid=(steps,),
             in_specs=[
-                pl.BlockSpec(kernels.shape, lambda i, *_: (0, 0)),
+                pl.BlockSpec(memory_space=pl.ANY),
+                pl.BlockSpec((1, size), lambda i, *_: (0, 0)),
+                pl.BlockSpec((size // 2, piece), lambda i, *_: (0, i)),
                 pl.BlockSpec(sky, lambda i, *_: (i, 0, 0)),
                 pl.BlockSpec(sky, lambda i, *_: (i, 1, 0)),
             ],
             out_specs=pl.BlockSpec((rows, pixels), lambda i, *_: (0, 0)),
             scratch_shapes=[
+                pltpu.SMEM((1, LANES), jnp.int32),
+                pltpu.SMEM((groups - 1, LANES), jnp.int32),
+                pltpu.VMEM((groups - 1, LANES), jnp.int32),
+                dma((2,)),
+                dma((groups - 1,)),
+                dma((groups - 1,)),
+                pltpu.VMEM((8, size), jnp.float32),
                 pltpu.VMEM((blocks, width, pixels), jnp.bfloat16),
-                pltpu.VMEM((width // LANES, delay_gain.shape[0], LANES), jnp.float32),
+                pltpu.VMEM((width // LANES, size, LANES), jnp.float32),
                 pltpu.VMEM((shards, chips, 2, rows, pixels), jnp.bfloat16),
                 pltpu.VMEM((shards, chips, rows, pixels), jnp.bfloat16),
                 pltpu.VMEM((shards, chips - 1, rows, pixels), jnp.bfloat16),
@@ -260,7 +308,7 @@
             collective_id=0, has_side_effects=True, vmem_limit_bytes=48 << 20
         ),
         name="stack_stamps",
-    )(every, by_column, kernels, sky_map, sky_map)
+    )(by_column, lists.reshape(1, LANES), delay_gain.reshape(1, size), cosine_table(size), sky_map, sky_map)
     return out[None]
 
 

time: 48.8 us -> 45.7 us (0.936)
  starting transfers between devices: 3.23 us -> 0 us
  local copies, waits for them, and re-layouts: 4.35 us -> 7.19 us
  matrix products: 2.77 us -> 0 us
  other arithmetic: 0.84 us -> 0 us
  Pallas kernels: 37.2 us -> 38 us
    unnamed x5 -> x9, local copies, waits for them, and re-layouts: 0.67 us -> 4.3 us
    ppermute x3 -> x0, starting transfers between devices: 3.23 us -> none  [body(): lax.ppermute(lists, 'chan', [(i, (i + e) % groups) for i in range(groups)])]
    dot_general x1 -> x0, matrix products: 2.77 us -> none  [filter_kernels(): jnp.dot(gains, table, precision=lax.Precision.HIGHEST, preferred_element_...]
    pallas_call x1, Pallas kernels: 35.6 us -> 36.4 us  [body(): pl.pallas_call(functools.partial(stack_kernel, groups, shards, slots, sta...]
    add x1 -> x0, other arithmetic: 0.76 us -> none  [filter_kernels(): gains = jnp.stack([even + odd, jnp.where(inside, even - odd, 0.0)])]
    slice x1 -> x0, local copies, waits for them, and re-layouts: 0.76 us -> none  [filter_kernels(): odd = jnp.pad(delay_gain[half + 1:], (1, 1))]
  transfers between devices with their start and end apart: 3 -> 0, of which waited for: 0 -> 0; matrix products, arithmetic and copies ran while one was open for 9% -> 0% of each run, Pallas kernels for 0% -> 0%
where the time goes in v3:
time: 45.7 us; the launch traced here: 45.2 us
  Pallas kernels  38 us (83%)
  local copies, waits for them, and re-layouts  7.19 us (16%)
    pallas_call x1, Pallas kernels, body(): pl.pallas_call(functools.partial(stack_kernel, groups, shards, slots, sta...  36.4 us
    unnamed x9, local copies, waits for them, and re-layouts  4.3 us
    pallas_call x1, Pallas kernels, body(): pl.pallas_call(resolve_kernel, out_shape=jax.ShapeDtypeStruct((LANES,), j...  1.6 us
    squeeze x1, local copies, waits for them, and re-layouts, body(): stamp_block[0, 0]  1.34 us
    squeeze x1, local copies, waits for them, and re-layouts, body(): chan_start[0, 0]  1.34 us

profile of v3, /device:TPU:0, one launch (start us, length us, event | category | flops | bytes accessed | tf_op | source)
XLA Modules:
  0.0 45.2 jit_solution(13122375322511333215)
XLA Ops:
  0.0 0.0 copy-start
  0.0 0.8 %copy-done = f32[8,4,8,2]{2,3,1,0:T(2,128)S(1)} copy-done((f32[8,4,8,2]{2,3,1,0:T(2,128)S(1)}, f32[8,4,8,2]{2,3,1,0:T(2,128)}, u32[]{:S(2)}) %copy-start) | copy-done | bytes 2072
  0.8 1.3 %copy.12.ranks_s = s32[8,2]{1,0:T(8,128)} copy(s32[8,2]{0,1:T(2,128)} %bitcast.10) | data formatting | bytes 128 | tf_op jit(solution)/shard_map/squeeze | solution.py:259
  2.1 1.3 %copy.13.starts_s = s32[8,2]{1,0:T(8,128)} copy(s32[8,2]{0,1:T(2,128)} %bitcast.11) | data formatting | bytes 128 | tf_op jit(solution)/shard_map/squeeze | solution.py:259
  3.4 1.6 %resolve_slots.1 = s32[128]{0:T(128)} custom-call(s32[32]{0:T(128)} %owner_s.1, s32[8,2]{1,0:T(8,128)} %copy.12.ranks_s, s32[8,2]{1,0:T(8,128)} %copy.13.starts_s), custom_call_target="tpu_custom_call" | custom-call | tf_op jit(solution)/shard_map/resolve_slots/pallas_call | solution.py:252
  5.1 0.1 copy.11
  5.2 0.1 reshape.10.over_s
  5.3 0.0 copy-start.1
  5.3 1.6 %copy-done.1 = f32[512,1024]{1,0:T(8,128)S(1)} copy-done((f32[512,1024]{1,0:T(8,128)S(1)}, f32[512,1024]{1,0:T(8,128)}, u32[]{:S(2)}) %copy-start.1) | copy-done | bytes 2097176
  6.9 0.0 copy-start.2
  6.9 0.7 %copy-done.2 = f32[1024]{0:T(1024)S(1)} copy-done((f32[1024]{0:T(1024)S(1)}, f32[1024]{0:T(1024)}, u32[]{:S(2)}) %copy-start.2) | copy-done | bytes 4120
  7.5 0.0 copy-start.3
  7.6 0.6 %copy-done.3 = s32[128]{0:T(128)S(1)} copy-done((s32[128]{0:T(128)S(1)}, s32[128]{0:T(128)}, u32[]{:S(2)}) %copy-start.3) | copy-done | bytes 536
  8.2 36.4 %stack_stamps.1 = f32[32,1024]{1,0:T(8,128)S(1)} custom-call(f32[64]{0:T(128)S(1)} %reshape.10.over_s, s32[1,128]{1,0:T(1,128)S(1)} %bitcast.9, f32[1,1024]{1,0:T(1,128)S(1)} %bitcast.8, f32[512,1024]{1,0:T(8,128)S(1)} %copy-done.1, bf16[256,32,1024]{2,1,0:T(8,128)(2,1)} %sky_b.1, bf16[256,32,1024]{2,1,0:T(8,128)(2,1)} %sky_b.1), custom_call_target="tpu_custom_call" | custom-call | tf_op jit(solution)/shard_map/stack_stamps/pallas_call | solution.py:268
  44.6 0.7 %copy.15 = f32[1,32,1024]{2,1,0:T(8,128)} copy(f32[1,32,1024]{2,1,0:T(8,128)S(1)} %bitcast.7) | data formatting | bytes 262144
  (1 shorter events, 0.0 us)
Async XLA Ops:
  0.0 0.8 %copy-start = (f32[8,4,8,2]{2,3,1,0:T(2,128)S(1)}, f32[8,4,8,2]{2,3,1,0:T(2,128)}, u32[]{:S(2)}) copy-start(f32[8,4,8,2]{2,3,1,0:T(2,128)} %param.11) | copy-start | bytes 6148
  5.3 1.6 %copy-start.1 = (f32[512,1024]{1,0:T(8,128)S(1)}, f32[512,1024]{1,0:T(8,128)}, u32[]{:S(2)}) copy-start(f32[512,1024]{1,0:T(8,128)} %constant.12.clone.table_ref) | copy-start | bytes 6291460
  6.9 0.7 %copy-start.2 = (f32[1024]{0:T(1024)S(1)}, f32[1024]{0:T(1024)}, u32[]{:S(2)}) copy-start(f32[1024]{0:T(1024)} %param.12) | copy-start | bytes 12292
  7.5 0.6 %copy-start.3 = (s32[128]{0:T(128)S(1)}, s32[128]{0:T(128)}, u32[]{:S(2)}) copy-start(s32[128]{0:T(128)} %resolve_slots.1) | copy-start | bytes 1540

commit v4 on v3

--- a/solution.py
+++ b/solution.py
@@ -11,8 +11,8 @@
 MESH = pl.DeviceIdType.MESH
 STEP = 32
 LANES = 128
-LAG1 = 2
-LAG2 = 4
+LAG1 = 1
+LAG2 = 3
 
 
 def cosine_table(size):
@@ -40,9 +40,8 @@
     return out + jnp.where(top, gain[:, half : half + 1] * sign, 0.0)
 
 
-def resolve_kernel(owner_s, ranks_s, starts_s, out_s, table):
+def resolve_kernel(shards, slots, owner_s, ranks_s, starts_s, out_s, table):
     c = lax.axis_index("chan")
-    shards, slots = ranks_s.shape
 
     def fill(b, count):
         table[count] = b
@@ -51,10 +50,10 @@
     count = lax.fori_loop(0, owner_s.shape[0], fill, jnp.int32(0))
     for q in range(shards):
         for s in range(slots):
-            rank = ranks_s[q, s]
+            rank = ranks_s[q * slots + s]
             live = (rank >= 0) & (rank < count)
             out_s[q * slots + s] = jnp.where(live, table[jnp.where(live, rank, 0)], -1)
-            out_s[(shards + q) * slots + s] = starts_s[q, s]
+            out_s[(shards + q) * slots + s] = starts_s[q * slots + s]
 
 
 def fill_filter(first, kernels_ref, filt):
@@ -250,13 +249,13 @@
 
     smem = pl.BlockSpec(memory_space=pltpu.SMEM)
     lists = pl.pallas_call(
-        resolve_kernel,
+        functools.partial(resolve_kernel, shards, slots),
         out_shape=jax.ShapeDtypeStruct((LANES,), jnp.int32),
         in_specs=[smem] * 3,
         out_specs=smem,
         scratch_shapes=[pltpu.SMEM((blocks + 1,), jnp.int32)],
         name="resolve_slots",
-    )(owner, stamp_block[0, 0], chan_start[0, 0])
+    )(owner, stamp_block.reshape(-1), chan_start.reshape(-1))
     by_column = lax.dynamic_index_in_dim(overdensity, p, 0, False).reshape(-1)
     step = min(STEP, width)
     steps = width // step

time: 45.7 us -> 45.1 us (0.987)
  Pallas kernels: 38 us -> 37.4 us
    squeeze x2 -> x0, local copies, waits for them, and re-layouts: 2.69 us -> none  [the longest x1 1.34 us: body(): stamp_block[0, 0]]
    unnamed x9 -> x11, local copies, waits for them, and re-layouts: 4.3 us -> 5.8 us
    reshape x0 -> x2, local copies, waits for them, and re-layouts: none -> 1.22 us  [the longest x1 0.62 us: body(): chan_start.reshape(-1)]
    pallas_call x1, Pallas kernels: 36.4 us -> 35.9 us  [body(): pl.pallas_call(functools.partial(stack_kernel, groups, shards, slots, sta...]
where the time goes in v4:
time: 45.1 us; the launch traced here: 44.7 us
  Pallas kernels  37.4 us (83%)
  local copies, waits for them, and re-layouts  7.22 us (16%)
    pallas_call x1, Pallas kernels, body(): pl.pallas_call(functools.partial(stack_kernel, groups, shards, slots, sta...  35.9 us
    unnamed x11, local copies, waits for them, and re-layouts  5.8 us
    pallas_call x1, Pallas kernels, body(): pl.pallas_call(functools.partial(resolve_kernel, shards, slots), out_shap...  1.49 us

profile of v4, /device:TPU:0, one launch (start us, length us, event | category | flops | bytes accessed | tf_op | source)
XLA Modules:
  0.0 44.7 jit_solution(4161294965823634294)
XLA Ops:
  0.0 0.0 copy-start
  0.0 0.8 %copy-done = f32[8,4,8,2]{2,3,1,0:T(2,128)S(1)} copy-done((f32[8,4,8,2]{2,3,1,0:T(2,128)S(1)}, f32[8,4,8,2]{2,3,1,0:T(2,128)}, u32[]{:S(2)}) %copy-start) | copy-done | bytes 2072
  0.8 0.8 %copy.12 = s32[1,1,8,2]{3,2,1,0:T(8,128)S(1)} copy(s32[1,1,8,2]{2,3,1,0:T(2,128)} %param.9) | data formatting | bytes 128 | tf_op args[2]
  1.5 0.6 %reshape.17.ranks_s = s32[16]{0:T(128)} reshape(s32[1,1,8,2]{3,2,1,0:T(8,128)S(1)} %copy.12) | data formatting | bytes 128 | tf_op jit(solution)/shard_map/reshape | solution.py:258
  2.1 0.8 %copy.13 = s32[1,1,8,2]{3,2,1,0:T(8,128)S(1)} copy(s32[1,1,8,2]{2,3,1,0:T(2,128)} %param.10) | data formatting | bytes 128 | tf_op args[3]
  2.9 0.6 %reshape.18.starts_s = s32[16]{0:T(128)} reshape(s32[1,1,8,2]{3,2,1,0:T(8,128)S(1)} %copy.13) | data formatting | bytes 128 | tf_op jit(solution)/shard_map/reshape | solution.py:258
  3.5 1.5 %resolve_slots.1 = s32[128]{0:T(128)} custom-call(s32[32]{0:T(128)} %owner_s.1, s32[16]{0:T(128)} %reshape.17.ranks_s, s32[16]{0:T(128)} %reshape.18.starts_s), custom_call_target="tpu_custom_call" | custom-call | tf_op jit(solution)/shard_map/resolve_slots/pallas_call | solution.py:251
  5.0 0.1 copy.11
  5.1 0.1 reshape.16.over_s
  5.2 0.0 copy-start.1
  5.2 1.6 %copy-done.1 = f32[512,1024]{1,0:T(8,128)S(1)} copy-done((f32[512,1024]{1,0:T(8,128)S(1)}, f32[512,1024]{1,0:T(8,128)}, u32[]{:S(2)}) %copy-start.1) | copy-done | bytes 2097176
  6.8 0.0 copy-start.2
  6.8 0.7 %copy-done.2 = f32[1024]{0:T(1024)S(1)} copy-done((f32[1024]{0:T(1024)S(1)}, f32[1024]{0:T(1024)}, u32[]{:S(2)}) %copy-start.2) | copy-done | bytes 4120
  7.5 0.0 copy-start.3
  7.5 0.6 %copy-done.3 = s32[128]{0:T(128)S(1)} copy-done((s32[128]{0:T(128)S(1)}, s32[128]{0:T(128)}, u32[]{:S(2)}) %copy-start.3) | copy-done | bytes 536
  8.1 35.9 %stack_stamps.1 = f32[32,1024]{1,0:T(8,128)S(1)} custom-call(f32[64]{0:T(128)S(1)} %reshape.16.over_s, s32[1,128]{1,0:T(1,128)S(1)} %bitcast.11, f32[1,1024]{1,0:T(1,128)S(1)} %bitcast.10, f32[512,1024]{1,0:T(8,128)S(1)} %copy-done.1, bf16[256,32,1024]{2,1,0:T(8,128)(2,1)} %sky_b.1, bf16[256,32,1024]{2,1,0:T(8,128)(2,1)} %sky_b.1), custom_call_target="tpu_custom_call" | custom-call | tf_op jit(solution)/shard_map/stack_stamps/pallas_call | solution.py:267
  44.0 0.7 %copy.15 = f32[1,32,1024]{2,1,0:T(8,128)} copy(f32[1,32,1024]{2,1,0:T(8,128)S(1)} %bitcast.9) | data formatting | bytes 262144
  (1 shorter events, 0.0 us)
Async XLA Ops:
  0.0 0.8 %copy-start = (f32[8,4,8,2]{2,3,1,0:T(2,128)S(1)}, f32[8,4,8,2]{2,3,1,0:T(2,128)}, u32[]{:S(2)}) copy-start(f32[8,4,8,2]{2,3,1,0:T(2,128)} %param.11) | copy-start | bytes 6148
  5.2 1.6 %copy-start.1 = (f32[512,1024]{1,0:T(8,128)S(1)}, f32[512,1024]{1,0:T(8,128)}, u32[]{:S(2)}) copy-start(f32[512,1024]{1,0:T(8,128)} %constant.12.clone.table_ref) | copy-start | bytes 6291460
  6.8 0.7 %copy-start.2 = (f32[1024]{0:T(1024)S(1)}, f32[1024]{0:T(1024)}, u32[]{:S(2)}) copy-start(f32[1024]{0:T(1024)} %param.12) | copy-start | bytes 12292
  7.5 0.6 %copy-start.3 = (s32[128]{0:T(128)S(1)}, s32[128]{0:T(128)}, u32[]{:S(2)}) copy-start(s32[128]{0:T(128)} %resolve_slots.1) | copy-start | bytes 1540
